TPU v7x, 32 devices: a whole 2x2x4 slice. The times are simulated.
32 devices in a mesh: dp: 16 (over z, y, core), shard: 2 (over x).
Axes of the slice: x: 2, y: 2, z: 4, core: 2. Of those that a mesh axis runs over, the one named last changes fastest.
Arguments:
- block_input: bfloat16 [4096, 1024], P(('dp', 'shard'))
- out_cotangent: bfloat16 [4096, 1024], P(('dp', 'shard')), may hold values from -6 to 6
- weight_input: float32 [1024, 3072], P('shard', 'dp'), may hold values from -0.1875 to 0.1875
- weight_output: float32 [1024, 1024], P('shard', 'dp'), may hold values from -0.1875 to 0.1875
- weight_gate: float32 [1024, 4608], P('shard', 'dp'), may hold values from -0.1875 to 0.1875
- weight_up: float32 [1024, 4608], P('shard', 'dp'), may hold values from -0.1875 to 0.1875
- weight_down: float32 [4608, 1024], P('shard', 'dp'), may hold values from -0.09375 to 0.09375
- conv_taps: float32 [3, 1024], P(None, 'shard'), may hold values from -3.5 to 3.5
- norm_gains: float32 [2, 1024], P(None, 'shard'), may hold values from 0.5 to 1.5
- first_input: float32 [1024, 3072], P('shard', 'dp'), may hold values from -20 to 20
- first_output: float32 [1024, 1024], P('shard', 'dp'), may hold values from -20 to 20
- first_gate: float32 [1024, 4608], P('shard', 'dp'), may hold values from -20 to 20
- first_up: float32 [1024, 4608], P('shard', 'dp'), may hold values from -20 to 20
- first_down: float32 [4608, 1024], P('shard', 'dp'), may hold values from -20 to 20
- first_taps: float32 [3, 1024], P(None, 'shard'), may hold values from -20 to 20
- first_gains: float32 [2, 1024], P(None, 'shard'), may hold values from -20 to 20
- second_input: float32 [1024, 3072], P('shard', 'dp'), may hold values from 20.48 to 122.88
- second_output: float32 [1024, 1024], P('shard', 'dp'), may hold values from 20.48 to 122.88
- second_gate: float32 [1024, 4608], P('shard', 'dp'), may hold values from 20.48 to 122.88
- second_up: float32 [1024, 4608], P('shard', 'dp'), may hold values from 20.48 to 122.88
- second_down: float32 [4608, 1024], P('shard', 'dp'), may hold values from 20.48 to 122.88
- second_taps: float32 [3, 1024], P(None, 'shard'), may hold values from 20.48 to 122.88
- second_gains: float32 [2, 1024], P(None, 'shard'), may hold values from 20.48 to 122.88
Outputs:
- block_output: bfloat16 [4096, 1024], P(('dp', 'shard'))
- input_gradient: float32 [4096, 1024], P(('dp', 'shard'))
- gradient_input: float32 [1024, 3072], P('shard', 'dp')
- gradient_output: float32 [1024, 1024], P('shard', 'dp')
- gradient_gate: float32 [1024, 4608], P('shard', 'dp')
- gradient_up: float32 [1024, 4608], P('shard', 'dp')
- gradient_down: float32 [4608, 1024], P('shard', 'dp')
- gradient_taps: float32 [3, 1024], P(None, 'shard')
- gradient_gains: float32 [2, 1024], P(None, 'shard')
- updated_input: float32 [1024, 3072], P('shard', 'dp')
- updated_output: float32 [1024, 1024], P('shard', 'dp')
- updated_gate: float32 [1024, 4608], P('shard', 'dp')
- updated_up: float32 [1024, 4608], P('shard', 'dp')
- updated_down: float32 [4608, 1024], P('shard', 'dp')
- updated_taps: float32 [3, 1024], P(None, 'shard')
- updated_gains: float32 [2, 1024], P(None, 'shard')
- moment_input: float32 [1024, 3072], P('shard', 'dp')
- moment_output: float32 [1024, 1024], P('shard', 'dp')
- moment_gate: float32 [1024, 4608], P('shard', 'dp')
- moment_up: float32 [1024, 4608], P('shard', 'dp')
- moment_down: float32 [4608, 1024], P('shard', 'dp')
- moment_taps: float32 [3, 1024], P(None, 'shard')
- moment_gains: float32 [2, 1024], P(None, 'shard')
- square_input: float32 [1024, 3072], P('shard', 'dp')
- square_output: float32 [1024, 1024], P('shard', 'dp')
- square_gate: float32 [1024, 4608], P('shard', 'dp')
- square_up: float32 [1024, 4608], P('shard', 'dp')
- square_down: float32 [4608, 1024], P('shard', 'dp')
- square_taps: float32 [3, 1024], P(None, 'shard')
- square_gains: float32 [2, 1024], P(None, 'shard')
All inputs are finite; a program needn't handle non-finite values.
Results may differ from a plain program's by a relative error of at most 0.00435.
The roundings to bfloat16 on the way count: a program that leaves them out, or rounds other values in their place, can miss the bound.
Values may be sent and summed in bfloat16 or wider, within the bound.
No kernel may reach another device: no remote copies, remote signals or barrier semaphores. Data moves between devices by JAX's collectives and lax.ppermute only.
A program may use at most 320 MiB of HBM per device.

v0:
```python
import jax
import jax.numpy as jnp
from jax import lax
from jax.sharding import PartitionSpec as P

D = 1024
KCONV = 3
LEN = 128
STEP = 10
epsilon_norm = 1e-05
epsilon_adam = 1e-08
beta_first = 0.9
beta_second = 0.95
rate_matrix = 0.01
rate_vector = 0.1
weight_decay = 0.1


def product(left, right):
    return jnp.dot(left, right, preferred_element_type=jnp.float32)


def times_transposed(left, right):
    return lax.dot_general(
        left, right, (((1,), (1,)), ((), ())), preferred_element_type=jnp.float32
    )


def transposed_times(left, right):
    return lax.dot_general(
        left, right, (((0,), (0,)), ((), ())), preferred_element_type=jnp.float32
    )


def delayed(values, steps):
    seqs = values.reshape(-1, LEN, values.shape[-1])
    padded = jnp.pad(seqs, ((0, 0), (steps, 0), (0, 0)))[:, :LEN]
    return padded.reshape(values.shape)


def advanced(values, steps):
    seqs = values.reshape(-1, LEN, values.shape[-1])
    padded = jnp.pad(seqs, ((0, 0), (0, steps), (0, 0)))[:, steps:]
    return padded.reshape(values.shape)


def norm_scale(values):
    return lax.rsqrt(jnp.mean(values * values, axis=1, keepdims=True) + epsilon_norm)


def norm_back(grad_in, normed, scale, gain):
    weighted = grad_in * gain
    return scale * (weighted - normed * jnp.mean(weighted * normed, axis=1, keepdims=True))


def reduce_weight(left, right):
    owned = lax.psum_scatter(
        transposed_times(left, right), "shard", scatter_dimension=0, tiled=True
    )
    return lax.psum_scatter(owned, "dp", scatter_dimension=1, tiled=True)


def adam_step(param, grad, moment, square, rate, decay):
    moment_new = beta_first * moment + (1.0 - beta_first) * grad
    square_new = beta_second * square + (1.0 - beta_second) * grad * grad
    corrected = moment_new / (1.0 - beta_first**STEP)
    spread = jnp.sqrt(square_new / (1.0 - beta_second**STEP))
    updated = param - rate * (corrected / (spread + epsilon_adam) + decay * param)
    return (updated, moment_new, square_new)


def shards(
    block_input,
    out_cotangent,
    weight_input,
    weight_output,
    weight_gate,
    weight_up,
    weight_down,
    conv_taps,
    norm_gains,
    first_input,
    first_output,
    first_gate,
    first_up,
    first_down,
    first_taps,
    first_gains,
    second_input,
    second_output,
    second_gate,
    second_up,
    second_down,
    second_taps,
    second_gains,
):
    columns = (
        lax.all_gather(weight_input.astype(jnp.bfloat16), "dp", axis=1, tiled=True),
        lax.all_gather(weight_output.astype(jnp.bfloat16), "dp", axis=1, tiled=True),
        lax.all_gather(weight_gate.astype(jnp.bfloat16), "dp", axis=1, tiled=True),
        lax.all_gather(weight_up.astype(jnp.bfloat16), "dp", axis=1, tiled=True),
        lax.all_gather(weight_down.astype(jnp.bfloat16), "dp", axis=1, tiled=True),
    )
    values = block_input.astype(jnp.float32)
    scale_one = norm_scale(values)
    normed_one = values * scale_one
    whole_input, whole_output, whole_gate, whole_up, whole_down, whole_taps, whole_gains = (
        lax.all_gather(columns[0], "shard", axis=0, tiled=True),
        lax.all_gather(columns[1], "shard", axis=0, tiled=True),
        lax.all_gather(columns[2], "shard", axis=0, tiled=True),
        lax.all_gather(columns[3], "shard", axis=0, tiled=True),
        lax.all_gather(columns[4], "shard", axis=0, tiled=True),
        lax.all_gather(conv_taps.astype(jnp.bfloat16), "shard", axis=1, tiled=True),
        lax.all_gather(norm_gains.astype(jnp.bfloat16), "shard", axis=1, tiled=True),
    )
    gains = whole_gains.astype(jnp.float32)
    taps = whole_taps.astype(jnp.float32)
    hidden_one = (normed_one * gains[0]).astype(jnp.bfloat16)
    projected = product(hidden_one, whole_input)
    input_gate = projected[:, :D]
    output_gate = projected[:, D : 2 * D]
    mixer_values = projected[:, 2 * D :]
    mixed_in = input_gate * mixer_values
    shifted = [delayed(mixed_in, step) for step in range(KCONV)]
    conv_out = taps[0] * shifted[0]
    for step in range(1, KCONV):
        conv_out = conv_out + taps[step] * shifted[step]
    gated = (output_gate * conv_out).astype(jnp.bfloat16)
    residual = values + product(gated, whole_output)
    scale_two = norm_scale(residual)
    normed_two = residual * scale_two
    hidden_two = (normed_two * gains[1]).astype(jnp.bfloat16)
    gate_pre = product(hidden_two, whole_gate)
    up_pre = product(hidden_two, whole_up)
    sigmoid_gate = jax.nn.sigmoid(gate_pre)
    silu_gate = gate_pre * sigmoid_gate
    activated = (silu_gate * up_pre).astype(jnp.bfloat16)
    block_output = (residual + product(activated, whole_down)).astype(jnp.bfloat16)
    act_grad = times_transposed(out_cotangent, whole_down)
    grad_down = reduce_weight(activated, out_cotangent)
    gate_grad = (act_grad * up_pre * sigmoid_gate * (1.0 + gate_pre * (1.0 - sigmoid_gate))).astype(
        jnp.bfloat16
    )
    up_grad = (act_grad * silu_gate).astype(jnp.bfloat16)
    grad_gate = reduce_weight(hidden_two, gate_grad)
    grad_up = reduce_weight(hidden_two, up_grad)
    hidden_two_grad = times_transposed(gate_grad, whole_gate) + times_transposed(up_grad, whole_up)
    gain_two_grad = jnp.sum(hidden_two_grad * normed_two, axis=0)
    residual_grad = out_cotangent.astype(jnp.float32) + norm_back(
        hidden_two_grad, normed_two, scale_two, gains[1]
    )
    residual_half = residual_grad.astype(jnp.bfloat16)
    grad_output = reduce_weight(gated, residual_half)
    gated_grad = times_transposed(residual_half, whole_output)
    conv_grad = gated_grad * output_gate
    mixed_grad = taps[0] * conv_grad
    for step in range(1, KCONV):
        mixed_grad = mixed_grad + taps[step] * advanced(conv_grad, step)
    taps_grad = jnp.stack([jnp.sum(conv_grad * shifted[step], axis=0) for step in range(KCONV)], 0)
    projected_grad = jnp.concatenate(
        [mixed_grad * mixer_values, gated_grad * conv_out, mixed_grad * input_gate], axis=1
    ).astype(jnp.bfloat16)
    grad_input = reduce_weight(hidden_one, projected_grad)
    hidden_one_grad = times_transposed(projected_grad, whole_input)
    gain_one_grad = jnp.sum(hidden_one_grad * normed_one, axis=0)
    input_gradient = residual_grad + norm_back(hidden_one_grad, normed_one, scale_one, gains[0])
    vector_terms = jnp.concatenate(
        [taps_grad, gain_one_grad[None, :], gain_two_grad[None, :]], axis=0
    )
    vector_owned = lax.psum_scatter(vector_terms, "shard", scatter_dimension=1, tiled=True)
    vector_total = lax.psum(vector_owned, "dp")
    grad_taps = vector_total[:KCONV]
    grad_gains = vector_total[KCONV:]
    params = (
        weight_input,
        weight_output,
        weight_gate,
        weight_up,
        weight_down,
        conv_taps,
        norm_gains,
    )
    grads = (grad_input, grad_output, grad_gate, grad_up, grad_down, grad_taps, grad_gains)
    firsts = (first_input, first_output, first_gate, first_up, first_down, first_taps, first_gains)
    seconds = (
        second_input,
        second_output,
        second_gate,
        second_up,
        second_down,
        second_taps,
        second_gains,
    )
    updated = []
    moments = []
    squares = []
    for index in range(7):
        rate = rate_matrix if index < 5 else rate_vector
        decay = weight_decay if index < 5 else 0.0
        result = adam_step(params[index], grads[index], firsts[index], seconds[index], rate, decay)
        updated.append(result[0])
        moments.append(result[1])
        squares.append(result[2])
    return (
        block_output,
        input_gradient,
        grads[0],
        grads[1],
        grads[2],
        grads[3],
        grads[4],
        grads[5],
        grads[6],
        updated[0],
        updated[1],
        updated[2],
        updated[3],
        updated[4],
        updated[5],
        updated[6],
        moments[0],
        moments[1],
        moments[2],
        moments[3],
        moments[4],
        moments[5],
        moments[6],
        squares[0],
        squares[1],
        squares[2],
        squares[3],
        squares[4],
        squares[5],
        squares[6],
    )


def solution(mesh):
    placed = (
        P(("dp", "shard"), None),
        P(("dp", "shard"), None),
        P("shard", "dp"),
        P("shard", "dp"),
        P("shard", "dp"),
        P("shard", "dp"),
        P("shard", "dp"),
        P(None, "shard"),
        P(None, "shard"),
        P("shard", "dp"),
        P("shard", "dp"),
        P("shard", "dp"),
        P("shard", "dp"),
        P("shard", "dp"),
        P(None, "shard"),
        P(None, "shard"),
        P("shard", "dp"),
        P("shard", "dp"),
        P("shard", "dp"),
        P("shard", "dp"),
        P("shard", "dp"),
        P(None, "shard"),
        P(None, "shard"),
    )
    return jax.shard_map(
        shards,
        mesh=mesh,
        in_specs=placed,
        out_specs=(
            P(("dp", "shard"), None),
            P(("dp", "shard"), None),
            P("shard", "dp"),
            P("shard", "dp"),
            P("shard", "dp"),
            P("shard", "dp"),
            P("shard", "dp"),
            P(None, "shard"),
            P(None, "shard"),
            P("shard", "dp"),
            P("shard", "dp"),
            P("shard", "dp"),
            P("shard", "dp"),
            P("shard", "dp"),
            P(None, "shard"),
            P(None, "shard"),
            P("shard", "dp"),
            P("shard", "dp"),
            P("shard", "dp"),
            P("shard", "dp"),
            P("shard", "dp"),
            P(None, "shard"),
            P(None, "shard"),
            P("shard", "dp"),
            P("shard", "dp"),
            P("shard", "dp"),
            P("shard", "dp"),
            P("shard", "dp"),
            P(None, "shard"),
            P(None, "shard"),
        ),
        check_vma=False,
    )
```

profile of v0, /device:TPU:0, one launch (start us, length us, event | category | flops | bytes accessed | tf_op | source)
XLA Modules:
  0.0 2118.9 jit_solution(6194754667816132566)
XLA Ops:
  14.3 44.8 %all-gather.11.cloned.1.call-done = bf16[512,3072]{0,1:T(8,128)(2,1)} async-done(((bf16[512,192]{0,1:T(8,128)(2,1)}), bf16[512,3072]{0,1:T(8,128)(2,1)}) %all-gather.11.cloned.1.call-update) | async-done | bytes 3145744 | tf_op jit(solution)/shard_map/all_gather | solution.py:98
  59.2 38.9 %all-gather.15.cloned.1.call-done = bf16[512,1024]{0,1:T(8,128)(2,1)} async-done(((bf16[512,64]{0,1:T(8,128)(2,1)}), bf16[512,1024]{0,1:T(8,128)(2,1)}) %all-gather.15.cloned.1.call-update) | async-done | bytes 1048592 | tf_op jit(solution)/shard_map/all_gather | solution.py:99
  98.1 54.9 %all-gather.23.cloned.1.call-done = bf16[512,4608]{0,1:T(8,128)(2,1)} async-done(((bf16[512,288]{0,1:T(8,128)(2,1)}), bf16[512,4608]{0,1:T(8,128)(2,1)}) %all-gather.23.cloned.1.call-update) | async-done | bytes 4718608 | tf_op jit(solution)/shard_map/all_gather | solution.py:101
  153.1 54.3 %all-gather.19.cloned.1.call-done = bf16[512,4608]{0,1:T(8,128)(2,1)} async-done(((bf16[512,288]{0,1:T(8,128)(2,1)}), bf16[512,4608]{0,1:T(8,128)(2,1)}) %all-gather.19.cloned.1.call-update) | async-done | bytes 4718608 | tf_op jit(solution)/shard_map/all_gather | solution.py:100
  207.5 54.3 %all-gather.27.cloned.1.call-done = bf16[2304,1024]{0,1:T(8,128)(2,1)} async-done(((bf16[2304,64]{0,1:T(8,128)(2,1)}), bf16[2304,1024]{0,1:T(8,128)(2,1)}) %all-gather.27.cloned.1.call-update) | async-done | bytes 4718608 | tf_op jit(solution)/shard_map/all_gather | solution.py:102
  271.5 70.7 %all-gather.13.cloned.1.call-done = bf16[1024,3072]{0,1:T(8,128)(2,1)} async-done(((bf16[512,3072]{0,1:T(8,128)(2,1)}), bf16[1024,3072]{0,1:T(8,128)(2,1)}) %all-gather.13.cloned.1.call-update) | async-done | bytes 6291472 | tf_op jit(solution)/shard_map/all_gather | solution.py:108
  349.1 27.8 %all-gather.17.cloned.1.call-done = bf16[1024,1024]{0,1:T(8,128)(2,1)} async-done(((bf16[512,1024]{0,1:T(8,128)(2,1)}), bf16[1024,1024]{0,1:T(8,128)(2,1)}) %all-gather.17.cloned.1.call-update) | async-done | bytes 2097168 | tf_op jit(solution)/shard_map/all_gather | solution.py:109
  379.5 116.9 %all-gather.25.cloned.1.call-done = bf16[1024,4608]{0,1:T(8,128)(2,1)} async-done(((bf16[512,4608]{0,1:T(8,128)(2,1)}), bf16[1024,4608]{0,1:T(8,128)(2,1)}) %all-gather.25.cloned.1.call-update) | async-done | bytes 9437200 | tf_op jit(solution)/shard_map/all_gather | solution.py:111
  504.7 111.3 %all-gather.21.cloned.1.call-done = bf16[1024,4608]{0,1:T(8,128)(2,1)} async-done(((bf16[512,4608]{0,1:T(8,128)(2,1)}), bf16[1024,4608]{0,1:T(8,128)(2,1)}) %all-gather.21.cloned.1.call-update) | async-done | bytes 9437200 | tf_op jit(solution)/shard_map/all_gather | solution.py:110
  624.3 111.1 %all-gather.29.cloned.1.call-done = bf16[4608,1024]{0,1:T(8,128)(2,1)} async-done(((bf16[2304,1024]{0,1:T(8,128)(2,1)}), bf16[4608,1024]{0,1:T(8,128)(2,1)}) %all-gather.29.cloned.1.call-update) | async-done | bytes 9437200 | tf_op jit(solution)/shard_map/all_gather | solution.py:112
  735.4 8.5 multiply_convert_fusion
  796.8 10.8 reduce-scatter.24.cloned.1.call-done
  810.6 143.7 %reduce-scatter.22.cloned.1.call-done = f32[512,3072]{1,0:T(8,128)} async-done(((f32[1024,3072]{1,0:T(8,128)}), f32[512,3072]{1,0:T(8,128)}) %reduce-scatter.22.cloned.1.call-update) | async-done | bytes 6291472 | tf_op jit(solution)/shard_map/reduce_scatter | solution.py:57
  960.9 207.5 %reduce-scatter.28.cloned.1.call-done = f32[512,4608]{1,0:T(8,128)} async-done(((f32[1024,4608]{1,0:T(8,128)}), f32[512,4608]{1,0:T(8,128)}) %reduce-scatter.28.cloned.1.call-update) | async-done | bytes 9437200 | tf_op jit(solution)/shard_map/reduce_scatter | solution.py:57
  1168.4 9.6 copy.159
  1178.1 204.3 %reduce-scatter.30.cloned.1.call-done = f32[2304,1024]{1,0:T(8,128)} async-done(((f32[4608,1024]{1,0:T(8,128)}), f32[2304,1024]{1,0:T(8,128)}) %reduce-scatter.30.cloned.1.call-update) | async-done | bytes 9437200 | tf_op jit(solution)/shard_map/reduce_scatter | solution.py:57
  1382.4 9.7 copy.161
  1392.3 204.0 %reduce-scatter.26.cloned.1.call-done = f32[512,4608]{1,0:T(8,128)} async-done(((f32[1024,4608]{1,0:T(8,128)}), f32[512,4608]{1,0:T(8,128)}) %reduce-scatter.26.cloned.1.call-update) | async-done | bytes 9437200 | tf_op jit(solution)/shard_map/reduce_scatter | solution.py:57
  1596.3 9.6 copy.157
  1615.7 61.4 %psum.7 = f32[5,512]{1,0:T(8,128)S(1)} all-reduce(f32[5,512]{1,0:T(8,128)} %reduce-scatter.32.cloned.1.call-done), channel_id=1, replica_groups=mesh['dp'=16,'shard'=2] {'dp'}, use_global_device_ids=true, to_apply=%region_20.21 | all-reduce | flops 2560 | bytes 20480 | tf_op jit(solution)/shard_map/psum | solution.py:171
  1680.1 83.4 %reduce-scatter.34.cloned.1.call-done = f32[192,512]{1,0:T(8,128)} async-done(((f32[3072,512]{1,0:T(8,128)}), f32[192,512]{1,0:T(8,128)}) %reduce-scatter.34.cloned.1.call-update) | async-done | bytes 393232
  1765.7 112.8 %reduce-scatter.40.cloned.1.call-done = f32[288,512]{1,0:T(8,128)} async-done(((f32[4608,512]{1,0:T(8,128)}), f32[288,512]{1,0:T(8,128)}) %reduce-scatter.40.cloned.1.call-update) | async-done | bytes 589840
  1881.1 112.8 %reduce-scatter.42.cloned.1.call-done = f32[64,2304]{1,0:T(8,128)} async-done(((f32[1024,2304]{1,0:T(8,128)}), f32[64,2304]{1,0:T(8,128)}) %reduce-scatter.42.cloned.1.call-update) | async-done | bytes 589840
  1996.5 113.0 %reduce-scatter.38.cloned.1.call-done = f32[288,512]{1,0:T(8,128)} async-done(((f32[4608,512]{1,0:T(8,128)}), f32[288,512]{1,0:T(8,128)}) %reduce-scatter.38.cloned.1.call-update) | async-done | bytes 589840
  (212 shorter events, 128.1 us)
Async XLA Ops:
  7.2 51.9 %all-gather.11.cloned.1.call-start = ((), (), s32[]{:S(2)}) async-start(), calls=%async_computation.11 | async-start | bytes 3342336 | tf_op jit(solution)/shard_map/all_gather | solution.py:98
  9.1 89.0 %all-gather.15.cloned.1.call-start = ((), (), s32[]{:S(2)}) async-start(), calls=%async_computation.13 | async-start | bytes 1114112 | tf_op jit(solution)/shard_map/all_gather | solution.py:99
  10.7 142.4 %all-gather.23.cloned.1.call-start = ((), (), s32[]{:S(2)}) async-start(), calls=%async_computation.17 | async-start | bytes 5013504 | tf_op jit(solution)/shard_map/all_gather | solution.py:101
  12.6 194.9 %all-gather.19.cloned.1.call-start = ((), (), s32[]{:S(2)}) async-start(), calls=%async_computation.15 | async-start | bytes 5013504 | tf_op jit(solution)/shard_map/all_gather | solution.py:100
  13.4 248.4 %all-gather.27.cloned.1.call-start = ((), (), s32[]{:S(2)}) async-start(), calls=%async_computation.19 | async-start | bytes 5013504 | tf_op jit(solution)/shard_map/all_gather | solution.py:102
  14.3 327.9 %all-gather.13.cloned.1.call-start = ((), (), s32[]{:S(2)}) async-start(), calls=%async_computation.12 | async-start | bytes 9437184 | tf_op jit(solution)/shard_map/all_gather | solution.py:108
  59.1 317.7 %all-gather.17.cloned.1.call-start = ((), (), s32[]{:S(2)}) async-start(), calls=%async_computation.14 | async-start | bytes 3145728 | tf_op jit(solution)/shard_map/all_gather | solution.py:109
  98.1 398.3 %all-gather.25.cloned.1.call-start = ((), (), s32[]{:S(2)}) async-start(), calls=%async_computation.18 | async-start | bytes 14155776 | tf_op jit(solution)/shard_map/all_gather | solution.py:111
  153.1 462.9 %all-gather.21.cloned.1.call-start = ((), (), s32[]{:S(2)}) async-start(), calls=%async_computation.16 | async-start | bytes 14155776 | tf_op jit(solution)/shard_map/all_gather | solution.py:110
  207.5 527.9 %all-gather.29.cloned.1.call-start = ((), (), s32[]{:S(2)}) async-start(), calls=%async_computation.20 | async-start | bytes 14155776 | tf_op jit(solution)/shard_map/all_gather | solution.py:112
  261.9 545.7 %reduce-scatter.24.cloned.1.call-start = ((), (), s32[]{:S(2)}) async-start(), calls=%async_computation.22 | async-start | bytes 6291456 | tf_op jit(solution)/shard_map/reduce_scatter | solution.py:57
  753.0 201.3 %reduce-scatter.22.cloned.1.call-start = ((), (), s32[]{:S(2)}) async-start(), calls=%async_computation.21 | async-start | bytes 18874368 | tf_op jit(solution)/shard_map/reduce_scatter | solution.py:57
  764.1 404.3 %reduce-scatter.28.cloned.1.call-start = ((), (), s32[]{:S(2)}) async-start(), calls=%async_computation.24 | async-start | bytes 28311552 | tf_op jit(solution)/shard_map/reduce_scatter | solution.py:57
  773.3 609.0 %reduce-scatter.30.cloned.1.call-start = ((), (), s32[]{:S(2)}) async-start(), calls=%async_computation.25 | async-start | bytes 28311552 | tf_op jit(solution)/shard_map/reduce_scatter | solution.py:57
  782.8 813.5 %reduce-scatter.26.cloned.1.call-start = ((), (), s32[]{:S(2)}) async-start(), calls=%async_computation.23 | async-start | bytes 28311552 | tf_op jit(solution)/shard_map/reduce_scatter | solution.py:57
  791.0 824.7 %reduce-scatter.32.cloned.1.call-start = ((), (), s32[]{:S(2)}) async-start(), calls=%async_computation.26 | async-start | bytes 49152 | tf_op jit(solution)/shard_map/reduce_scatter | solution.py:170
  796.7 881.7 %reduce-scatter.36.cloned.1.call-start = ((), (), s32[]{:S(2)}) async-start(), calls=%async_computation.28 | async-start | bytes 2228224
  810.6 952.9 %reduce-scatter.34.cloned.1.call-start = ((), (), s32[]{:S(2)}) async-start(), calls=%async_computation.27 | async-start | bytes 6684672
  960.9 917.6 %reduce-scatter.40.cloned.1.call-start = ((), (), s32[]{:S(2)}) async-start(), calls=%async_computation.30 | async-start | bytes 10027008
  1178.0 815.9 %reduce-scatter.42.cloned.1.call-start = ((), (), s32[]{:S(2)}) async-start(), calls=%async_computation.31 | async-start | bytes 10027008
  1392.0 717.5 %reduce-scatter.38.cloned.1.call-start = ((), (), s32[]{:S(2)}) async-start(), calls=%async_computation.29 | async-start | bytes 10027008
  1615.7 262.9 %copy-start.11 = (f32[512,288]{0,1:T(8,128)S(1)}, f32[512,288]{0,1:T(8,128)}, u32[]{:S(2)}) copy-start(f32[512,288]{0,1:T(8,128)} %param.28) | copy-start | bytes 1769476
  1615.7 262.9 %copy-start.27 = (f32[512,288]{0,1:T(8,128)S(1)}, f32[512,288]{0,1:T(8,128)}, u32[]{:S(2)}) copy-start(f32[512,288]{0,1:T(8,128)} %param.35) | copy-start | bytes 1769476
  1615.7 262.9 %copy-start.28 = (f32[512,288]{0,1:T(8,128)S(1)}, f32[512,288]{0,1:T(8,128)}, u32[]{:S(2)}) copy-start(f32[512,288]{0,1:T(8,128)} %param.42) | copy-start | bytes 1769476
  (57 other events, 3002.9 us)
Sparse Core Ops, SparseCore 0:
  10.9 48.1 all-gather.10
  61.8 36.1 all-gather.14
  100.9 52.0 all-gather.22
  155.8 51.6 all-gather.18
  210.2 51.6 all-gather.26
  263.3 78.8 all-gather.12
  343.7 33.0 all-gather.16
  378.4 117.9 all-gather.24
  498.0 117.9 all-gather.20
  617.4 117.9 all-gather.28
  753.2 54.3 reduce-scatter.23
  809.7 144.5 reduce-scatter.21
  956.6 211.7 reduce-scatter.27
  1170.6 211.7 reduce-scatter.29
  1384.5 211.7 reduce-scatter.25
  1598.9 9.9 reduce-scatter.31
  1613.1 62.0 reduce-scatter.35
  1679.5 83.9 reduce-scatter.33
  1768.2 110.3 reduce-scatter.39
  1883.1 110.8 reduce-scatter.41
  1998.6 110.8 reduce-scatter.37
where the time goes:
time: 2120 us
  waiting for transfers between devices  1880 us (89%)
  matrix products  84.4 us (4%)
  blocking collectives  70.1 us (3%)
  local copies, waits for them, and re-layouts  48.5 us (2%)
  other arithmetic  22.4 us (1%)
    reduce_scatter x5, waiting for transfers between devices, reduce_weight(): lax.psum_scatter(transposed_times(left, right), 'shard', scatter_dimensio...  770 us
    unnamed x26, waiting for transfers between devices  422 us
    all_gather x1, waiting for transfers between devices, shards(): lax.all_gather(columns[3], 'shard', axis=0, tiled=True)  117 us
    all_gather x1, waiting for transfers between devices, shards(): lax.all_gather(columns[2], 'shard', axis=0, tiled=True)  111 us
    all_gather x1, waiting for transfers between devices, shards(): lax.all_gather(columns[4], 'shard', axis=0, tiled=True)  111 us
    all_gather x1, waiting for transfers between devices, shards(): lax.all_gather(columns[0], 'shard', axis=0, tiled=True)  70.7 us
    psum x1, blocking collectives, shards(): vector_total = lax.psum(vector_owned, 'dp')  61.4 us
    all_gather x1, waiting for transfers between devices, shards(): lax.all_gather(weight_up.astype(jnp.bfloat16), 'dp', axis=1, tiled=True)  54.9 us
  transfers between devices with their start and end apart: 21, of which 19 were waited for; matrix products, arithmetic and copies ran while one was open for 6% of the time, Pallas kernels for 0%

commit v1 on v0

--- a/solution.py
+++ b/solution.py
@@ -14,6 +14,18 @@
 rate_matrix = 0.01
 rate_vector = 0.1
 weight_decay = 0.1
+
+
+def collect(x, axis, dim):
+    ways, here, step = (lax.axis_size(axis), lax.axis_index(axis), x.shape[dim])
+    line, have = (x, 1)
+    while have < ways:
+        line = jnp.concatenate(
+            [line, lax.ppermute(line, axis, [(d, (d - have) % ways) for d in range(ways)])],
+            axis=dim,
+        )
+        have = 2 * have
+    return jnp.roll(line, here * step, axis=dim)
 
 
 def product(left, right):
@@ -108,7 +120,7 @@
         lax.all_gather(columns[0], "shard", axis=0, tiled=True),
         lax.all_gather(columns[1], "shard", axis=0, tiled=True),
         lax.all_gather(columns[2], "shard", axis=0, tiled=True),
-        lax.all_gather(columns[3], "shard", axis=0, tiled=True),
+        collect(columns[3], "shard", 0),
         lax.all_gather(columns[4], "shard", axis=0, tiled=True),
         lax.all_gather(conv_taps.astype(jnp.bfloat16), "shard", axis=1, tiled=True),
         lax.all_gather(norm_gains.astype(jnp.bfloat16), "shard", axis=1, tiled=True),

time: 2120 us -> 2090 us (0.986)
  waiting for transfers between devices: 1880 us -> 1650 us
  blocking collectives: 70.1 us -> 249 us
    all_gather x1, blocking collectives: 4.35 us -> 183 us  [shards(): lax.all_gather(norm_gains.astype(jnp.bfloat16), 'shard', axis=1, tiled=True)]
    all_gather x1 -> x0, waiting for transfers between devices: 117 us -> none  [shards(): lax.all_gather(columns[3], 'shard', axis=0, tiled=True)]
    all_gather x1, waiting for transfers between devices: 70.7 us -> 0.02 us  [shards(): lax.all_gather(columns[0], 'shard', axis=0, tiled=True)]
    all_gather x1, waiting for transfers between devices: 27.8 us -> 0.01 us  [shards(): lax.all_gather(columns[1], 'shard', axis=0, tiled=True)]
    unnamed x125 -> x117, local copies, waits for them, and re-layouts: 47.8 us -> 44.9 us
    unnamed x26 -> x25, waiting for transfers between devices: 422 us -> 422 us
  transfers between devices with their start and end apart: 21 -> 21, of which waited for: 19 -> 16; matrix products, arithmetic and copies ran while one was open for 6% -> 6% of each run, Pallas kernels for 0% -> 0%
where the time goes in v1:
time: 2090 us
  waiting for transfers between devices  1650 us (79%)
  blocking collectives  249 us (12%)
  matrix products  87.4 us (4%)
  local copies, waits for them, and re-layouts  45.5 us (2%)
  other arithmetic  35.5 us (2%)
    reduce_scatter x5, waiting for transfers between devices, reduce_weight(): lax.psum_scatter(transposed_times(left, right), 'shard', scatter_dimensio...  771 us
    unnamed x25, waiting for transfers between devices  422 us
    all_gather x1, blocking collectives, shards(): lax.all_gather(norm_gains.astype(jnp.bfloat16), 'shard', axis=1, tiled=True)  183 us
    all_gather x1, waiting for transfers between devices, shards(): lax.all_gather(columns[4], 'shard', axis=0, tiled=True)  111 us
    all_gather x1, waiting for transfers between devices, shards(): lax.all_gather(columns[2], 'shard', axis=0, tiled=True)  101 us
    psum x1, blocking collectives, shards(): vector_total = lax.psum(vector_owned, 'dp')  61.4 us
    all_gather x1, waiting for transfers between devices, shards(): lax.all_gather(weight_gate.astype(jnp.bfloat16), 'dp', axis=1, tiled=True)  54.9 us
    all_gather x1, waiting for transfers between devices, shards(): lax.all_gather(weight_down.astype(jnp.bfloat16), 'dp', axis=1, tiled=True)  54.3 us
  transfers between devices with their start and end apart: 21, of which 16 were waited for; matrix products, arithmetic and copies ran while one was open for 6% of the time, Pallas kernels for 0%

profile of v1, /device:TPU:0, one launch (start us, length us, event | category | flops | bytes accessed | tf_op | source)
XLA Modules:
  0.0 2087.1 jit_solution(15367808874646614422)
XLA Ops:
  14.3 44.8 %all-gather.10.cloned.1.call-done = bf16[512,3072]{0,1:T(8,128)(2,1)} async-done(((bf16[512,192]{0,1:T(8,128)(2,1)}), bf16[512,3072]{0,1:T(8,128)(2,1)}) %all-gather.10.cloned.1.call-update) | async-done | bytes 3145744 | tf_op jit(solution)/shard_map/all_gather | solution.py:110
  59.2 38.9 %all-gather.14.cloned.1.call-done = bf16[512,1024]{0,1:T(8,128)(2,1)} async-done(((bf16[512,64]{0,1:T(8,128)(2,1)}), bf16[512,1024]{0,1:T(8,128)(2,1)}) %all-gather.14.cloned.1.call-update) | async-done | bytes 1048592 | tf_op jit(solution)/shard_map/all_gather | solution.py:111
  98.1 54.9 %all-gather.18.cloned.1.call-done = bf16[512,4608]{0,1:T(8,128)(2,1)} async-done(((bf16[512,288]{0,1:T(8,128)(2,1)}), bf16[512,4608]{0,1:T(8,128)(2,1)}) %all-gather.18.cloned.1.call-update) | async-done | bytes 4718608 | tf_op jit(solution)/shard_map/all_gather | solution.py:112
  153.1 54.3 %all-gather.24.cloned.1.call-done = bf16[2304,1024]{0,1:T(8,128)(2,1)} async-done(((bf16[2304,64]{0,1:T(8,128)(2,1)}), bf16[2304,1024]{0,1:T(8,128)(2,1)}) %all-gather.24.cloned.1.call-update) | async-done | bytes 4718608 | tf_op jit(solution)/shard_map/all_gather | solution.py:114
  207.5 54.3 %all-gather.22.cloned.1.call-done = bf16[512,4608]{0,1:T(8,128)(2,1)} async-done(((bf16[512,288]{0,1:T(8,128)(2,1)}), bf16[512,4608]{0,1:T(8,128)(2,1)}) %all-gather.22.cloned.1.call-update) | async-done | bytes 4718608 | tf_op jit(solution)/shard_map/all_gather | solution.py:113
  263.4 183.1 %all_gather.33 = bf16[2,1024]{1,0:T(2,128)(2,1)S(1)} all-gather(bf16[2,512]{1,0:T(2,128)(2,1)S(1)} %convert_element_type.67), channel_id=1, replica_groups=mesh['dp'=16,'shard'=2] {'shard'}, dimensions={1}, use_global_device_ids=true | all-gather | bytes 6144 | tf_op jit(solution)/shard_map/all_gather | solution.py:126
  460.7 12.5 fusion.2
  473.2 101.2 %all-gather.20.cloned.1.call-done = bf16[1024,4608]{0,1:T(8,128)(2,1)} async-done(((bf16[512,4608]{0,1:T(8,128)(2,1)}), bf16[1024,4608]{0,1:T(8,128)(2,1)}) %all-gather.20.cloned.1.call-update) | async-done | bytes 9437200 | tf_op jit(solution)/shard_map/all_gather | solution.py:122
  574.4 8.3 fusion.53
  582.7 111.2 %all-gather.26.cloned.1.call-done = bf16[4608,1024]{0,1:T(8,128)(2,1)} async-done(((bf16[2304,1024]{0,1:T(8,128)(2,1)}), bf16[4608,1024]{0,1:T(8,128)(2,1)}) %all-gather.26.cloned.1.call-update) | async-done | bytes 9437200 | tf_op jit(solution)/shard_map/all_gather | solution.py:124
  700.6 9.2 multiply_convert_fusion
  764.9 10.9 reduce-scatter.24.cloned.1.call-done
  778.8 143.9 %reduce-scatter.22.cloned.1.call-done = f32[512,3072]{1,0:T(8,128)} async-done(((f32[1024,3072]{1,0:T(8,128)}), f32[512,3072]{1,0:T(8,128)}) %reduce-scatter.22.cloned.1.call-update) | async-done | bytes 6291472 | tf_op jit(solution)/shard_map/reduce_scatter | solution.py:69
  929.3 207.3 %reduce-scatter.28.cloned.1.call-done = f32[512,4608]{1,0:T(8,128)} async-done(((f32[1024,4608]{1,0:T(8,128)}), f32[512,4608]{1,0:T(8,128)}) %reduce-scatter.28.cloned.1.call-update) | async-done | bytes 9437200 | tf_op jit(solution)/shard_map/reduce_scatter | solution.py:69
  1136.6 9.6 copy.159
  1146.3 204.4 %reduce-scatter.26.cloned.1.call-done = f32[512,4608]{1,0:T(8,128)} async-done(((f32[1024,4608]{1,0:T(8,128)}), f32[512,4608]{1,0:T(8,128)}) %reduce-scatter.26.cloned.1.call-update) | async-done | bytes 9437200 | tf_op jit(solution)/shard_map/reduce_scatter | solution.py:69
  1350.7 9.6 copy.157
  1360.4 204.2 %reduce-scatter.30.cloned.1.call-done = f32[2304,1024]{1,0:T(8,128)} async-done(((f32[4608,1024]{1,0:T(8,128)}), f32[2304,1024]{1,0:T(8,128)}) %reduce-scatter.30.cloned.1.call-update) | async-done | bytes 9437200 | tf_op jit(solution)/shard_map/reduce_scatter | solution.py:69
  1564.7 9.6 copy.161
  1584.0 61.4 %psum.7 = f32[5,512]{1,0:T(8,128)S(1)} all-reduce(f32[5,512]{1,0:T(8,128)} %reduce-scatter.32.cloned.1.call-done), channel_id=1, replica_groups=mesh['dp'=16,'shard'=2] {'dp'}, use_global_device_ids=true, to_apply=%region_20.21 | all-reduce | flops 2560 | bytes 20480 | tf_op jit(solution)/shard_map/psum | solution.py:183
  1648.5 83.3 %reduce-scatter.34.cloned.1.call-done = f32[192,512]{1,0:T(8,128)} async-done(((f32[3072,512]{1,0:T(8,128)}), f32[192,512]{1,0:T(8,128)}) %reduce-scatter.34.cloned.1.call-update) | async-done | bytes 393232
  1734.3 112.5 %reduce-scatter.40.cloned.1.call-done = f32[288,512]{1,0:T(8,128)} async-done(((f32[4608,512]{1,0:T(8,128)}), f32[288,512]{1,0:T(8,128)}) %reduce-scatter.40.cloned.1.call-update) | async-done | bytes 589840
  1849.5 112.8 %reduce-scatter.38.cloned.1.call-done = f32[288,512]{1,0:T(8,128)} async-done(((f32[4608,512]{1,0:T(8,128)}), f32[288,512]{1,0:T(8,128)}) %reduce-scatter.38.cloned.1.call-update) | async-done | bytes 589840
  1965.1 112.6 %reduce-scatter.42.cloned.1.call-done = f32[64,2304]{1,0:T(8,128)} async-done(((f32[1024,2304]{1,0:T(8,128)}), f32[64,2304]{1,0:T(8,128)}) %reduce-scatter.42.cloned.1.call-update) | async-done | bytes 589840
  (204 shorter events, 117.2 us)
Async XLA Ops:
  7.2 51.9 %all-gather.10.cloned.1.call-start = ((), (), s32[]{:S(2)}) async-start(), calls=%async_computation.11 | async-start | bytes 3342336 | tf_op jit(solution)/shard_map/all_gather | solution.py:110
  9.1 89.0 %all-gather.14.cloned.1.call-start = ((), (), s32[]{:S(2)}) async-start(), calls=%async_computation.13 | async-start | bytes 1114112 | tf_op jit(solution)/shard_map/all_gather | solution.py:111
  10.7 142.4 %all-gather.18.cloned.1.call-start = ((), (), s32[]{:S(2)}) async-start(), calls=%async_computation.15 | async-start | bytes 5013504 | tf_op jit(solution)/shard_map/all_gather | solution.py:112
  12.6 194.9 %all-gather.24.cloned.1.call-start = ((), (), s32[]{:S(2)}) async-start(), calls=%async_computation.18 | async-start | bytes 5013504 | tf_op jit(solution)/shard_map/all_gather | solution.py:114
  13.4 248.4 %all-gather.22.cloned.1.call-start = ((), (), s32[]{:S(2)}) async-start(), calls=%async_computation.17 | async-start | bytes 5013504 | tf_op jit(solution)/shard_map/all_gather | solution.py:113
  14.3 437.2 %all-gather.12.cloned.1.call-start = ((), (), s32[]{:S(2)}) async-start(), calls=%async_computation.12 | async-start | bytes 9437184 | tf_op jit(solution)/shard_map/all_gather | solution.py:120
  59.1 398.5 %all-gather.16.cloned.1.call-start = ((), (), s32[]{:S(2)}) async-start(), calls=%async_computation.14 | async-start | bytes 3145728 | tf_op jit(solution)/shard_map/all_gather | solution.py:121
  98.1 476.3 %all-gather.20.cloned.1.call-start = ((), (), s32[]{:S(2)}) async-start(), calls=%async_computation.16 | async-start | bytes 14155776 | tf_op jit(solution)/shard_map/all_gather | solution.py:122
  153.1 540.9 %all-gather.26.cloned.1.call-start = ((), (), s32[]{:S(2)}) async-start(), calls=%async_computation.19 | async-start | bytes 14155776 | tf_op jit(solution)/shard_map/all_gather | solution.py:124
  207.5 243.8 %copy-start.4 = (bf16[128,1024]{1,0:T(8,128)(2,1)S(1)}, bf16[128,1024]{1,0:T(8,128)(2,1)}, u32[]{:S(2)}) copy-start(bf16[128,1024]{1,0:T(8,128)(2,1)} %param.23) | copy-start | bytes 786436
  207.5 568.3 %reduce-scatter.24.cloned.1.call-start = ((), (), s32[]{:S(2)}) async-start(), calls=%async_computation.21 | async-start | bytes 6291456 | tf_op jit(solution)/shard_map/reduce_scatter | solution.py:69
  261.9 198.5 %collective-permute-start = (bf16[512,4608]{0,1:T(8,128)(2,1)}, bf16[512,4608]{0,1:T(8,128)(2,1)}, u32[]{:S(2)}, u32[]{:S(2)}) collective-permute-start(bf16[512,4608]{0,1:T(8,128)(2,1)} %all-gather.22.cloned.1.call-done), channel_id=1, source_target_pairs={{0,1},{1,0},{2,3},{3,2},{4,5},{5,4},{6,7},{7,6},{8,9},{9,8},{10,11... | collective-permute-start | bytes 14155784 | tf_op jit(solution)/shard_map/ppermute | solution.py:24
  721.3 201.4 %reduce-scatter.22.cloned.1.call-start = ((), (), s32[]{:S(2)}) async-start(), calls=%async_computation.20 | async-start | bytes 18874368 | tf_op jit(solution)/shard_map/reduce_scatter | solution.py:69
  732.4 404.3 %reduce-scatter.28.cloned.1.call-start = ((), (), s32[]{:S(2)}) async-start(), calls=%async_computation.23 | async-start | bytes 28311552 | tf_op jit(solution)/shard_map/reduce_scatter | solution.py:69
  741.7 609.1 %reduce-scatter.26.cloned.1.call-start = ((), (), s32[]{:S(2)}) async-start(), calls=%async_computation.22 | async-start | bytes 28311552 | tf_op jit(solution)/shard_map/reduce_scatter | solution.py:69
  749.9 814.8 %reduce-scatter.30.cloned.1.call-start = ((), (), s32[]{:S(2)}) async-start(), calls=%async_computation.24 | async-start | bytes 28311552 | tf_op jit(solution)/shard_map/reduce_scatter | solution.py:69
  759.2 824.8 %reduce-scatter.32.cloned.1.call-start = ((), (), s32[]{:S(2)}) async-start(), calls=%async_computation.25 | async-start | bytes 49152 | tf_op jit(solution)/shard_map/reduce_scatter | solution.py:182
  764.9 881.9 %reduce-scatter.36.cloned.1.call-start = ((), (), s32[]{:S(2)}) async-start(), calls=%async_computation.27 | async-start | bytes 2228224
  778.7 953.1 %reduce-scatter.34.cloned.1.call-start = ((), (), s32[]{:S(2)}) async-start(), calls=%async_computation.26 | async-start | bytes 6684672
  929.3 917.5 %reduce-scatter.40.cloned.1.call-start = ((), (), s32[]{:S(2)}) async-start(), calls=%async_computation.29 | async-start | bytes 10027008
  1146.3 816.1 %reduce-scatter.38.cloned.1.call-start = ((), (), s32[]{:S(2)}) async-start(), calls=%async_computation.28 | async-start | bytes 10027008
  1360.4 717.4 %reduce-scatter.42.cloned.1.call-start = ((), (), s32[]{:S(2)}) async-start(), calls=%async_computation.30 | async-start | bytes 10027008
  1584.0 262.7 %copy-start.14 = (f32[512,288]{0,1:T(8,128)S(1)}, f32[512,288]{0,1:T(8,128)}, u32[]{:S(2)}) copy-start(f32[512,288]{0,1:T(8,128)} %param.28) | copy-start | bytes 1769476
  1584.0 262.7 %copy-start.28 = (f32[512,288]{0,1:T(8,128)S(1)}, f32[512,288]{0,1:T(8,128)}, u32[]{:S(2)}) copy-start(f32[512,288]{0,1:T(8,128)} %param.35) | copy-start | bytes 1769476
  (53 other events, 2433.9 us)
Sparse Core Ops, SparseCore 0:
  10.9 48.1 all-gather.9
  61.8 36.1 all-gather.13
  100.9 52.0 all-gather.17
  155.8 51.6 all-gather.23
  210.2 51.6 all-gather.21
  263.3 146.3 all-gather.11
  411.2 45.0 all-gather.15
  457.9 116.5 all-gather.19
  576.0 117.9 all-gather.25
  721.4 54.3 reduce-scatter.23
  778.1 144.5 reduce-scatter.21
  924.9 211.7 reduce-scatter.27
  1138.9 211.7 reduce-scatter.25
  1352.9 211.7 reduce-scatter.29
  1567.3 9.9 reduce-scatter.31
  1581.5 61.8 reduce-scatter.35
  1647.8 84.0 reduce-scatter.33
  1736.4 110.3 reduce-scatter.39
  1851.4 110.8 reduce-scatter.37
  1966.9 110.8 reduce-scatter.41
